TPU v7x, 128 devices: a whole 4x4x4 slice. The times are simulated.
128 devices in a mesh: ctx: 32 (over z, x, core), head: 4 (over y).
Axes of the slice: x: 4, y: 4, z: 4, core: 2. Of those that a mesh axis runs over, the one named last changes fastest.
Arguments:
- queries: bfloat16 [16384, 4096], P('ctx', 'head'), may hold values from -8 to 8
- keys: bfloat16 [16384, 512], P('ctx', 'head'), may hold values from -8 to 8
- values: bfloat16 [16384, 512], P('ctx', 'head'), may hold values from -6 to 6
- distances: int32 [4, 3], P('head'), may hold values from 1 to 31, as said below
- out_weight: bfloat16 [4096, 2048], P('head'), may hold values from -0.09375 to 0.09375
- residual: bfloat16 [16384, 2048], P(('ctx', 'head')), may hold values from -6 to 6
- norm_gain: float32 [2048], replicated, may hold values from 0.25 to 1.75
- expert_gate_up: bfloat16 [128, 2048, 1536], P(('ctx', 'head')), may hold values from -0.125 to 0.125
- expert_down: bfloat16 [128, 768, 2048], P(('ctx', 'head')), may hold values from -0.21875 to 0.21875
- routes: int32 [16384, 8], P(('ctx', 'head')), may hold values from 0 to 127, all different within a row; in each aligned block of 128 rows (0 to 127, 128 to 255, ...) at most 16 rows name the same one
- route_weights: float32 [16384, 8], P(('ctx', 'head')), may hold values from 0.05 to 0.5
Outputs:
- attended: bfloat16 [16384, 2048], P(('ctx', 'head'))
- moe_out: bfloat16 [16384, 2048], P(('ctx', 'head'))
Inputs may be any that keep to these rules, and one draw needn't show every extreme that they name: Each row holds 3 different distances; some row holds the distance 16384 // 1024. `routes`: among the 128 rows of one device, no expert is named by more than 16 rows.
All inputs are finite; a program needn't handle non-finite values.
Results may differ from a plain program's by a relative error of at most 0.01.
Values may be sent and summed in bfloat16 or wider, within the bound.
No kernel may reach another device: no remote copies, remote signals or barrier semaphores. Data moves between devices by JAX's collectives and lax.ppermute only.
A program may use at most 128 MiB of HBM per device.

v0:
```python
import math
import jax
import jax.numpy as jnp
from jax import lax
from jax.sharding import PartitionSpec as P

HD = 128
FFE = 768
TOP = 8
EXP_DEV = 1
BLK = 128
DIST = 3


def expert_rows(arrived, expert_gate_up, expert_down, sources):
    width = arrived.shape[2]
    grid = arrived.reshape(sources, EXP_DEV, arrived.shape[1], width)
    projected = jnp.einsum(
        "sekd,edf->eskf", grid, expert_gate_up, preferred_element_type=jnp.float32
    )
    hidden = (jax.nn.silu(projected[..., :FFE]) * projected[..., FFE:]).astype(jnp.bfloat16)
    output = jnp.einsum("eskf,efd->sekd", hidden, expert_down, preferred_element_type=jnp.float32)
    return output.astype(jnp.bfloat16).reshape(arrived.shape)


def body(
    queries,
    keys,
    values,
    distances,
    out_weight,
    residual,
    norm_gain,
    expert_gate_up,
    expert_down,
    routes,
    route_weights,
):
    length = queries.shape[0]
    groups = queries.shape[1] // HD
    blocks = length // BLK
    scale = 1.0 / math.sqrt(HD)
    wanted = distances[0]
    source = lax.axis_index("ctx") - wanted
    usable = source >= 0
    packed = jnp.concatenate([keys, values], axis=1)
    everything = lax.all_gather(packed, "ctx", axis=0, tiled=True)
    offsets = jnp.maximum(source, 0) * length
    fetched = jnp.stack(
        [
            lax.dynamic_slice_in_dim(everything, offsets[slot_index], length, 0)
            for slot_index in range(DIST)
        ]
    )
    query = queries.reshape(length, groups, HD)
    causal = jnp.arange(length)[:, None] >= jnp.arange(length)[None, :]
    local = jnp.einsum("tgd,ud->gtu", query, keys, preferred_element_type=jnp.float32) * scale
    local = jnp.where(causal[None], local, -jnp.inf)
    far_keys = fetched[:, :, :HD].reshape(DIST, blocks, BLK, HD)
    far_values = fetched[:, :, HD:].reshape(DIST, blocks, BLK, HD)
    query_blocks = queries.reshape(blocks, BLK, groups, HD)
    remote = (
        jnp.einsum("bqgd,jbud->gjbqu", query_blocks, far_keys, preferred_element_type=jnp.float32)
        * scale
    )
    remote = jnp.where(usable[None, :, None, None, None], remote, -jnp.inf)
    highest = jnp.maximum(local.max(-1), remote.max(axis=(1, 4)).reshape(groups, length))
    near_weight = jnp.exp(local - highest[:, :, None])
    far_weight = jnp.exp(remote - highest.reshape(groups, blocks, BLK)[:, None, :, :, None])
    denominator = near_weight.sum(-1) + far_weight.sum(axis=(1, 4)).reshape(groups, length)
    mixed = jnp.einsum(
        "gtu,ud->tgd", near_weight.astype(jnp.bfloat16), values, preferred_element_type=jnp.float32
    )
    far_mixed = jnp.einsum(
        "gjbqu,jbud->bqgd",
        far_weight.astype(jnp.bfloat16),
        far_values,
        preferred_element_type=jnp.float32,
    )
    mixed = mixed + far_mixed.reshape(length, groups, HD)
    attention = (
        (mixed / jnp.transpose(denominator)[:, :, None])
        .astype(jnp.bfloat16)
        .reshape(length, groups * HD)
    )
    summed = lax.psum_scatter(
        jnp.dot(attention, out_weight, preferred_element_type=jnp.float32),
        "head",
        scatter_dimension=0,
        tiled=True,
    )
    attended = (residual.astype(jnp.float32) + summed).astype(jnp.bfloat16)
    widened = attended.astype(jnp.float32)
    inverse = lax.rsqrt(jnp.mean(widened * widened, axis=-1, keepdims=True) + 1e-06)
    normed = (widened * inverse * norm_gain).astype(jnp.bfloat16)
    local_rows = normed.shape[0]
    width = normed.shape[1]
    devices = lax.axis_size(("ctx", "head"))
    experts = devices * EXP_DEV
    capacity = max(2, 2 * local_rows * TOP // experts)
    flat_experts = routes.reshape(local_rows * TOP)
    onehot = (flat_experts[:, None] == jnp.arange(experts, dtype=jnp.int32)[None, :]).astype(
        jnp.int32
    )
    places = jnp.sum(jnp.cumsum(onehot, axis=0) * onehot, axis=1) - 1
    owners = jnp.arange(local_rows * TOP, dtype=jnp.int32) // TOP
    outgoing = (
        jnp.zeros((experts, capacity, width), jnp.bfloat16)
        .at[flat_experts, places]
        .set(normed[owners])
    )
    answered = expert_rows(
        lax.all_to_all(outgoing, ("ctx", "head"), split_axis=0, concat_axis=0, tiled=True),
        expert_gate_up,
        expert_down,
        devices,
    )
    returned = lax.all_to_all(answered, ("ctx", "head"), split_axis=0, concat_axis=0, tiled=True)
    picked = returned[flat_experts, places].astype(jnp.float32)
    weighted = route_weights.reshape(local_rows * TOP)[:, None] * picked
    moe_out = weighted.reshape(local_rows, TOP, width).sum(axis=1).astype(jnp.bfloat16)
    return (attended, moe_out)


def solution(mesh):
    return jax.shard_map(
        body,
        mesh=mesh,
        in_specs=(
            P("ctx", "head"),
            P("ctx", "head"),
            P("ctx", "head"),
            P("head", None),
            P("head", None),
            P(("ctx", "head"), None),
            P(),
            P(("ctx", "head"), None, None),
            P(("ctx", "head"), None, None),
            P(("ctx", "head"), None),
            P(("ctx", "head"), None),
        ),
        out_specs=(P(("ctx", "head"), None), P(("ctx", "head"), None)),
        check_vma=False,
    )
```

profile of v0, /device:TPU:7, one launch (start us, length us, event | category | flops | bytes accessed | tf_op | source)
XLA Modules:
  0.0 481.5 jit_solution(17237951945180817351)
XLA Ops:
  7.2 1.9 pad_maximum_fusion.1
  14.4 2.6 copy.69
  19.7 2.3 bitcast_bitcast_fusion
  21.9 6.0 %fusion.8 = (f32[8,512]{1,0:T(8,128)S(1)}, f32[512,512,8]{1,0,2:T(8,128)}) fusion(pred[512,512]{0,1:T(8,128)(4,1)S(1)} %iota_compare_fusion, bf16[512,128]{1,0:T(8,128)(2,1)} %param.12, bf16[512,1024]{1,0:T(8,128)(2,1)} %param.11), kind=kOutput, calls=%fused_computation.12 | convolution fusion | flops 543158272 | bytes 9846784 | tf_op jit(solution)/shard_map/tgd,ud->gtu/dot_general | solution.py:57
  27.9 38.7 %all-gather.2.cloned.1.call-done = bf16[16384,256]{1,0:T(8,128)(2,1)} async-done(((bf16[512,256]{1,0:T(8,128)(2,1)}), bf16[16384,256]{1,0:T(8,128)(2,1)}) %all-gather.2.cloned.1.call-update) | async-done | bytes 8388624 | tf_op jit(solution)/shard_map/all_gather | solution.py:47
  68.3 2.2 bitcast_reduce_fusion
  70.5 2.2 fusion.12
  72.7 2.5 fusion.27
  75.2 3.2 copy.44
  78.4 3.1 reshape.226
  81.5 5.3 %fusion.3 = f32[8,512]{1,0:T(8,128)S(1)} fusion(f32[512,512,8]{1,0,2:T(8,128)} %get-tuple-element.22, f32[8,512]{1,0:T(8,128)S(1)} %bitcast_maximum_fusion.1, pred[512,512]{0,1:T(8,128)(4,1)S(1)} %iota_compare_fusion), kind=kLoop, calls=%fused_computation.9 | loop fusion | flops 8384512 | bytes 8683520 | tf_op jit(solution)/shard_map/reduce_sum | solution.py:70
  86.8 5.7 %fusion.26 = bf16[512,8,128]{0,2,1:T(8,128)(2,1)S(1)} fusion(f32[512,8,128]{0,2,1:T(8,128)S(1)} %copy-done.4, f32[512,512,8]{1,0,2:T(8,128)} %get-tuple-element.22, f32[8,512]{1,0:T(8,128)S(1)} %bitcast_maximum_fusion.1, pred[512,512]{0,1:T(8,128)(4,1)S(1)} %iota_compare_fusion, f32[512,8]{0,1:T(8,128)S(1)} %fusion.48, bf16[512,128]{1,0:T(8,128)(2,1)S(1)} %copy-done.5), kind=kOutput, calls=%fused_computation.34 | convolution fusion | flops 546832384 | bytes 11960320 | tf_op jit(solution)/shard_map/gtu,ud->tgd/dot_general | solution.py:71
  92.5 4.4 fusion.54
  100.3 42.7 %reduce-scatter.2.cloned.1.call-done = f32[128,2048]{1,0:T(8,128)} async-done(((f32[512,2048]{1,0:T(8,128)}), f32[128,2048]{1,0:T(8,128)}) %reduce-scatter.2.cloned.1.call-update) | async-done | bytes 1048592 | tf_op jit(solution)/shard_map/reduce_scatter | solution.py:86
  143.0 1.6 fusion.32
  146.4 26.0 %scatter_custom_fusion = bf16[2048,2048]{1,0:T(8,128)(2,1)} fusion(s32[1024]{0:T(1024)S(1)} %get-tuple-element.24, bf16[128,2048]{1,0:T(8,128)(2,1)} %fusion.34, s32[1024]{0:T(1024)S(1)} %get-tuple-element.23, bf16[]{:T(256)} %constant.49.clone.1), kind=kCustom, calls=%fused_computation.23 | custom fusion | bytes 8389120
  172.4 104.5 %all_to_all.10 = bf16[128,16,2048]{2,1,0:T(8,128)(2,1)S(1)} all-to-all(bf16[128,16,2048]{2,1,0:T(8,128)(2,1)} %bitcast.117), channel_id=1, replica_groups=mesh['ctx'=32,'head'=4] {'ctx','head'}, dimensions={0} | all-to-all | bytes 16777216 | tf_op jit(solution)/shard_map/all_to_all | solution.py:113
  276.9 35.8 %fusion.5 = f32[1,128,16,1536]{3,1,2,0:T(8,128)S(1)} fusion(bf16[128,16,2048]{2,1,0:T(8,128)(2,1)S(1)} %all_to_all.10, bf16[1,2048,1536]{2,1,0:T(8,128)(2,1)} %param.18), kind=kOutput, calls=%fused_computation.11 | convolution fusion | flops 12884901888 | bytes 27262976 | tf_op jit(solution)/shard_map/sekd,edf->eskf/dot_general | solution.py:18
  312.7 9.0 %convolution_convert_fusion = bf16[128,16,2048]{2,0,1:T(8,128)(2,1)} fusion(bf16[1,768,2048]{2,1,0:T(8,128)(2,1)S(1)} %copy-done, f32[1,128,16,1536]{3,1,2,0:T(8,128)S(1)} %fusion.5), kind=kOutput, calls=%fused_computation.20 | convolution fusion | flops 6456082432 | bytes 24117248 | tf_op jit(solution)/shard_map/eskf,efd->sekd/dot_general | solution.py:22
  321.7 11.2 %copy.52 = bf16[128,16,2048]{2,1,0:T(8,128)(2,1)} copy(bf16[128,16,2048]{2,0,1:T(8,128)(2,1)} %convolution_convert_fusion) | data formatting | bytes 16777216 | tf_op jit(solution)/shard_map/convert_element_type | solution.py:23
  332.9 6.9 %all-to-all-start.1 = ((bf16[128,16,2048]{2,1,0:T(8,128)(2,1)}), bf16[128,16,2048]{2,1,0:T(8,128)(2,1)}, u32[]{:S(2)}, u32[]{:S(2)}) async-start(bf16[128,16,2048]{2,1,0:T(8,128)(2,1)} %copy.52), calls=%async_computation.2 | async-start | bytes 16777216 | tf_op jit(solution)/shard_map/all_to_all | solution.py:118
  339.9 101.4 %all-to-all-done.1 = bf16[128,16,2048]{2,1,0:T(8,128)(2,1)} async-done(((bf16[128,16,2048]{2,1,0:T(8,128)(2,1)}), bf16[128,16,2048]{2,1,0:T(8,128)(2,1)}, u32[]{:S(2)}, u32[]{:S(2)}) %all-to-all-start.1) | async-done | bytes 8388640 | tf_op jit(solution)/shard_map/all_to_all | solution.py:118
  441.3 25.6 %gather_fusion = bf16[1024,2048]{1,0:T(8,128)(2,1)} fusion(bf16[128,16,2048]{2,1,0:T(8,128)(2,1)} %all-to-all-done.1, s32[1024]{0:T(1024)S(1)} %bitcast.116), kind=kCustom, calls=%fused_computation.1 | custom fusion | bytes 8396800 | tf_op jit(solution)/shard_map/gather | solution.py:119
  466.9 7.3 %fusion = bf16[128,2048]{1,0:T(8,128)(2,1)} fusion(bf16[1024,2048]{1,0:T(8,128)(2,1)} %gather_fusion, f32[128,8]{1,0:T(8,128)S(1)} %copy.45), kind=kLoop, calls=%fused_computation.4 | loop fusion | flops 6029312 | bytes 4722688 | tf_op jit(solution)/shard_map/reduce_sum | solution.py:121
  (59 shorter events, 9.0 us)
Async XLA Ops:
  7.2 305.6 %copy-start = (bf16[1,768,2048]{2,1,0:T(8,128)(2,1)S(1)}, bf16[1,768,2048]{2,1,0:T(8,128)(2,1)}, u32[]{:S(2)}) copy-start(bf16[1,768,2048]{2,1,0:T(8,128)(2,1)} %param.19) | copy-start | bytes 9437188
  7.2 59.5 %all-gather.2.cloned.1.call-start = ((), (), s32[]{:S(2)}) async-start(), calls=%async_computation.3 | async-start | bytes 8650752 | tf_op jit(solution)/shard_map/all_gather | solution.py:47
  9.1 133.9 %reduce-scatter.2.cloned.1.call-start = ((), (), s32[]{:S(2)}) async-start(), calls=%async_computation.4 | async-start | bytes 5242880 | tf_op jit(solution)/shard_map/reduce_scatter | solution.py:86
  78.4 8.4 %copy-start.5 = (bf16[512,128]{1,0:T(8,128)(2,1)S(1)}, bf16[512,128]{1,0:T(8,128)(2,1)}, u32[]{:S(2)}) copy-start(bf16[512,128]{1,0:T(8,128)(2,1)} %param.13) | copy-start | bytes 393220
  81.5 5.3 %copy-start.6 = (f32[8,4,128]{2,0,1:T(8,128)S(1)}, f32[8,4,128]{2,0,1:T(8,128)}, u32[]{:S(2)}) copy-start(f32[8,4,128]{2,0,1:T(8,128)} %get-tuple-element.9) | copy-start | bytes 49156
  81.5 5.3 %copy-start.4 = (f32[512,8,128]{0,2,1:T(8,128)S(1)}, f32[512,8,128]{0,2,1:T(8,128)}, u32[]{:S(2)}) copy-start(f32[512,8,128]{0,2,1:T(8,128)} %reshape.226) | copy-start | bytes 6291460
  86.8 5.7 %copy-start.1 = (bf16[1024,2048]{1,0:T(8,128)(2,1)S(1)}, bf16[1024,2048]{1,0:T(8,128)(2,1)}, u32[]{:S(2)}) copy-start(bf16[1024,2048]{1,0:T(8,128)(2,1)} %param.15) | copy-start | bytes 12582916
  92.5 4.4 copy-start.8
  96.9 3.2 copy-start.11
  96.9 3.3 copy-start.10
  96.9 48.5 %copy-start.7 = (f32[2048]{0:T(1024)S(1)}, f32[2048]{0:T(1024)}, u32[]{:S(2)}) copy-start(f32[2048]{0:T(1024)} %param.17) | copy-start | bytes 24580
  97.6 0.8 copy-start.2
  144.6 0.8 copy-start.3
  332.9 6.9 %copy-start.9 = (f32[128,8]{0,1:T(8,128)S(1)}, f32[128,8]{0,1:T(8,128)}, u32[]{:S(2)}) copy-start(f32[128,8]{0,1:T(8,128)} %param.21) | copy-start | bytes 12292
  332.9 108.4 %all-to-all-start.1 = ((bf16[128,16,2048]{2,1,0:T(8,128)(2,1)}), bf16[128,16,2048]{2,1,0:T(8,128)(2,1)}, u32[]{:S(2)}, u32[]{:S(2)}) async-start(bf16[128,16,2048]{2,1,0:T(8,128)(2,1)} %copy.52), calls=%async_computation.2 | async-start | bytes 16777216 | tf_op jit(solution)/shard_map/all_to_all | solution.py:118
Sparse Core Ops, SparseCore 0:
  10.8 55.7 all-gather.1
  97.1 45.8 reduce-scatter.1
where the time goes:
time: 488 us; the launch traced here: 481 us
  waiting for transfers between devices  183 us (38%)
  blocking collectives  105 us (22%)
  local copies, waits for them, and re-layouts  78.4 us (16%)
  matrix products  65.6 us (13%)
  other arithmetic  22.6 us (5%)
  between operations  20.6 us (4%)
  starting transfers between devices  6.97 us (1%)
    all_to_all x1, blocking collectives, body(): lax.all_to_all(outgoing, ('ctx', 'head'), split_axis=0, concat_axis=0, ti...  105 us
    all_to_all x1, waiting for transfers between devices, body(): lax.all_to_all(answered, ('ctx', 'head'), split_axis=0, concat_axis=0, ti...  101 us
    reduce_scatter x1, waiting for transfers between devices, body(): lax.psum_scatter(jnp.dot(attention, out_weight, preferred_element_type=jn...  42.7 us
    all_gather x1, waiting for transfers between devices, body(): everything = lax.all_gather(packed, 'ctx', axis=0, tiled=True)  38.7 us
    dot_general x1, matrix products, expert_rows(): jnp.einsum('sekd,edf->eskf', grid, expert_gate_up, preferred_element_type...  35.8 us
    unnamed x28, local copies, waits for them, and re-layouts  30.4 us
    gather x1, local copies, waits for them, and re-layouts, body(): picked = returned[flat_experts, places].astype(jnp.float32)  25.6 us
    convert_element_type x1, local copies, waits for them, and re-layouts, expert_rows(): return output.astype(jnp.bfloat16).reshape(arrived.shape)  11.2 us
  transfers between devices with their start and end apart: 3, of which 3 were waited for; matrix products, arithmetic and copies ran while one was open for 3% of the time, Pallas kernels for 0%

commit v1 on v0

--- a/solution.py
+++ b/solution.py
@@ -44,7 +44,9 @@
     source = lax.axis_index("ctx") - wanted
     usable = source >= 0
     packed = jnp.concatenate([keys, values], axis=1)
-    everything = lax.all_gather(packed, "ctx", axis=0, tiled=True)
+    everything = jnp.concatenate(
+        lax.all_to_all(jnp.stack([packed] * lax.axis_size("ctx")), "ctx", 0, 0), axis=0
+    )
     offsets = jnp.maximum(source, 0) * length
     fetched = jnp.stack(
         [

time: 488 us -> 547 us (1.12)
  waiting for transfers between devices: 183 us -> 229 us
  starting transfers between devices: 6.97 us -> 15.9 us
    all_to_all x0 -> x1, waiting for transfers between devices: none -> 83.4 us  [body(): lax.all_to_all(jnp.stack([packed] * lax.axis_size('ctx')), 'ctx', 0, 0)]
    all_gather x1 -> x0, waiting for transfers between devices: 38.7 us -> none  [body(): everything = lax.all_gather(packed, 'ctx', axis=0, tiled=True)]
    all_to_all x0 -> x1, starting transfers between devices: none -> 8.91 us  [body(): lax.all_to_all(jnp.stack([packed] * lax.axis_size('ctx')), 'ctx', 0, 0)]
    unnamed x28 -> x36, local copies, waits for them, and re-layouts: 30.4 us -> 30 us
where the time goes in v1:
time: 547 us; the launch traced here: 540 us
  waiting for transfers between devices  229 us (42%)
  blocking collectives  105 us (19%)
  local copies, waits for them, and re-layouts  82.2 us (15%)
  matrix products  65.4 us (12%)
  other arithmetic  21.7 us (4%)
  between operations  20.7 us (4%)
  starting transfers between devices  15.9 us (3%)
    all_to_all x1, blocking collectives, body(): lax.all_to_all(outgoing, ('ctx', 'head'), split_axis=0, concat_axis=0, ti...  105 us
    all_to_all x1, waiting for transfers between devices, body(): lax.all_to_all(answered, ('ctx', 'head'), split_axis=0, concat_axis=0, ti...  101 us
    all_to_all x1, waiting for transfers between devices, body(): lax.all_to_all(jnp.stack([packed] * lax.axis_size('ctx')), 'ctx', 0, 0)  83.4 us
    reduce_scatter x1, waiting for transfers between devices, body(): lax.psum_scatter(jnp.dot(attention, out_weight, preferred_element_type=jn...  44.4 us
    dot_general x1, matrix products, expert_rows(): jnp.einsum('sekd,edf->eskf', grid, expert_gate_up, preferred_element_type...  35.8 us
    unnamed x36, local copies, waits for them, and re-layouts  30 us
    gather x1, local copies, waits for them, and re-layouts, body(): picked = returned[flat_experts, places].astype(jnp.float32)  25.6 us
    convert_element_type x1, local copies, waits for them, and re-layouts, expert_rows(): return output.astype(jnp.bfloat16).reshape(arrived.shape)  11.2 us
  transfers between devices with their start and end apart: 3, of which 3 were waited for; matrix products, arithmetic and copies ran while one was open for 3% of the time, Pallas kernels for 0%

profile of v1, /device:TPU:7, one launch (start us, length us, event | category | flops | bytes accessed | tf_op | source)
XLA Modules:
  0.0 539.7 jit_solution(18380346977950944823)
XLA Ops:
  8.3 4.2 stack.10
  12.5 8.9 %all-to-all-start = ((bf16[32,512,256]{2,1,0:T(8,128)(2,1)}), bf16[32,512,256]{2,1,0:T(8,128)(2,1)}, u32[]{:S(2)}, u32[]{:S(2)}) async-start(bf16[32,512,256]{2,1,0:T(8,128)(2,1)} %stack.10), calls=%async_computation | async-start | bytes 16777216 | tf_op jit(solution)/shard_map/all_to_all | solution.py:48
  26.1 2.5 copy.69
  31.2 2.4 bitcast_bitcast_fusion
  33.6 5.9 %fusion.8 = (f32[8,512]{1,0:T(8,128)S(1)}, f32[512,512,8]{1,0,2:T(8,128)}) fusion(pred[512,512]{0,1:T(8,128)(4,1)S(1)} %iota_compare_fusion, bf16[512,128]{1,0:T(8,128)(2,1)S(1)} %copy-done.5, bf16[512,1024]{1,0:T(8,128)(2,1)} %param.11), kind=kOutput, calls=%fused_computation.12 | convolution fusion | flops 543158272 | bytes 9846784 | tf_op jit(solution)/shard_map/tgd,ud->gtu/dot_general | solution.py:59
  39.5 83.4 %all-to-all-done = bf16[32,512,256]{2,1,0:T(8,128)(2,1)} async-done(((bf16[32,512,256]{2,1,0:T(8,128)(2,1)}), bf16[32,512,256]{2,1,0:T(8,128)(2,1)}, u32[]{:S(2)}, u32[]{:S(2)}) %all-to-all-start) | async-done | bytes 8388640 | tf_op jit(solution)/shard_map/all_to_all | solution.py:48
  124.5 2.2 bitcast_reduce_fusion
  127.3 2.2 fusion.12
  129.6 2.5 fusion.27
  132.0 3.2 copy.44
  135.2 3.1 reshape.232
  138.3 5.3 fusion.3
  143.6 5.7 %fusion.26 = bf16[512,8,128]{0,2,1:T(8,128)(2,1)S(1)} fusion(f32[512,8,128]{0,2,1:T(8,128)S(1)} %copy-done.4, f32[512,512,8]{1,0,2:T(8,128)} %get-tuple-element.22, f32[8,512]{1,0:T(8,128)S(1)} %copy-done.7, pred[512,512]{0,1:T(8,128)(4,1)S(1)} %iota_compare_fusion, f32[512,8]{0,1:T(8,128)S(1)} %fusion.48, bf16[512,128]{1,0:T(8,128)(2,1)S(1)} %copy-done.6), kind=kOutput, calls=%fused_computation.34 | convolution fusion | flops 546832384 | bytes 11960320 | tf_op jit(solution)/shard_map/gtu,ud->tgd/dot_general | solution.py:73
  149.3 4.4 fusion.54
  157.1 44.4 %reduce-scatter.2.cloned.1.call-done = f32[128,2048]{1,0:T(8,128)} async-done(((f32[512,2048]{1,0:T(8,128)}), f32[128,2048]{1,0:T(8,128)}) %reduce-scatter.2.cloned.1.call-update) | async-done | bytes 1048592 | tf_op jit(solution)/shard_map/reduce_scatter | solution.py:88
  204.9 25.7 %scatter_custom_fusion = bf16[2048,2048]{1,0:T(8,128)(2,1)} fusion(s32[1024]{0:T(1024)S(1)} %get-tuple-element.24, bf16[128,2048]{1,0:T(8,128)(2,1)} %fusion.34, s32[1024]{0:T(1024)S(1)} %get-tuple-element.23, bf16[]{:T(256)} %constant.49.clone.1), kind=kCustom, calls=%fused_computation.23 | custom fusion | bytes 8389120
  230.6 104.5 %all_to_all.15 = bf16[128,16,2048]{2,1,0:T(8,128)(2,1)S(1)} all-to-all(bf16[128,16,2048]{2,1,0:T(8,128)(2,1)} %bitcast.118), channel_id=1, replica_groups=mesh['ctx'=32,'head'=4] {'ctx','head'}, dimensions={0} | all-to-all | bytes 16777216 | tf_op jit(solution)/shard_map/all_to_all | solution.py:115
  335.1 35.8 %fusion.5 = f32[1,128,16,1536]{3,1,2,0:T(8,128)S(1)} fusion(bf16[128,16,2048]{2,1,0:T(8,128)(2,1)S(1)} %all_to_all.15, bf16[1,2048,1536]{2,1,0:T(8,128)(2,1)} %param.18), kind=kOutput, calls=%fused_computation.11 | convolution fusion | flops 12884901888 | bytes 27262976 | tf_op jit(solution)/shard_map/sekd,edf->eskf/dot_general | solution.py:18
  370.9 8.9 %convolution_convert_fusion = bf16[128,16,2048]{2,0,1:T(8,128)(2,1)} fusion(bf16[1,768,2048]{2,1,0:T(8,128)(2,1)S(1)} %copy-done, f32[1,128,16,1536]{3,1,2,0:T(8,128)S(1)} %fusion.5), kind=kOutput, calls=%fused_computation.20 | convolution fusion | flops 6456082432 | bytes 24117248 | tf_op jit(solution)/shard_map/eskf,efd->sekd/dot_general | solution.py:22
  379.9 11.2 %copy.52 = bf16[128,16,2048]{2,1,0:T(8,128)(2,1)} copy(bf16[128,16,2048]{2,0,1:T(8,128)(2,1)} %convolution_convert_fusion) | data formatting | bytes 16777216 | tf_op jit(solution)/shard_map/convert_element_type | solution.py:23
  391.1 6.9 %all-to-all-start.2 = ((bf16[128,16,2048]{2,1,0:T(8,128)(2,1)}), bf16[128,16,2048]{2,1,0:T(8,128)(2,1)}, u32[]{:S(2)}, u32[]{:S(2)}) async-start(bf16[128,16,2048]{2,1,0:T(8,128)(2,1)} %copy.52), calls=%async_computation.3 | async-start | bytes 16777216 | tf_op jit(solution)/shard_map/all_to_all | solution.py:120
  398.1 101.4 %all-to-all-done.2 = bf16[128,16,2048]{2,1,0:T(8,128)(2,1)} async-done(((bf16[128,16,2048]{2,1,0:T(8,128)(2,1)}), bf16[128,16,2048]{2,1,0:T(8,128)(2,1)}, u32[]{:S(2)}, u32[]{:S(2)}) %all-to-all-start.2) | async-done | bytes 8388640 | tf_op jit(solution)/shard_map/all_to_all | solution.py:120
  499.5 25.6 %gather_fusion = bf16[1024,2048]{1,0:T(8,128)(2,1)} fusion(bf16[128,16,2048]{2,1,0:T(8,128)(2,1)} %all-to-all-done.2, s32[1024]{0:T(1024)S(1)} %bitcast.117), kind=kCustom, calls=%fused_computation.1 | custom fusion | bytes 8396800 | tf_op jit(solution)/shard_map/gather | solution.py:121
  525.1 7.3 %fusion = bf16[128,2048]{1,0:T(8,128)(2,1)} fusion(bf16[1024,2048]{1,0:T(8,128)(2,1)} %gather_fusion, f32[128,8]{1,0:T(8,128)S(1)} %copy.45), kind=kLoop, calls=%fused_computation.4 | loop fusion | flops 6029312 | bytes 4722688 | tf_op jit(solution)/shard_map/reduce_sum | solution.py:123
  (67 shorter events, 11.5 us)
Async XLA Ops:
  7.2 363.8 %copy-start = (bf16[1,768,2048]{2,1,0:T(8,128)(2,1)S(1)}, bf16[1,768,2048]{2,1,0:T(8,128)(2,1)}, u32[]{:S(2)}) copy-start(bf16[1,768,2048]{2,1,0:T(8,128)(2,1)} %param.19) | copy-start | bytes 9437188
  12.5 9.0 %copy-start.15 = (s32[1,3]{1,0:T(1,128)S(1)}, s32[1,3]{1,0:T(1,128)}, u32[]{:S(2)}) copy-start(s32[1,3]{1,0:T(1,128)} %param.14) | copy-start | bytes 40
  12.5 21.1 %copy-start.5 = (bf16[512,128]{1,0:T(8,128)(2,1)S(1)}, bf16[512,128]{1,0:T(8,128)(2,1)}, u32[]{:S(2)}) copy-start(bf16[512,128]{1,0:T(8,128)(2,1)} %param.12) | copy-start | bytes 393220
  12.5 110.4 %all-to-all-start = ((bf16[32,512,256]{2,1,0:T(8,128)(2,1)}), bf16[32,512,256]{2,1,0:T(8,128)(2,1)}, u32[]{:S(2)}, u32[]{:S(2)}) async-start(bf16[32,512,256]{2,1,0:T(8,128)(2,1)} %stack.10), calls=%async_computation | async-start | bytes 16777216 | tf_op jit(solution)/shard_map/all_to_all | solution.py:48
  21.4 180.1 %reduce-scatter.2.cloned.1.call-start = ((), (), s32[]{:S(2)}) async-start(), calls=%async_computation.4 | async-start | bytes 5242880 | tf_op jit(solution)/shard_map/reduce_scatter | solution.py:88
  124.3 3.0 copy-start.10
  129.6 8.7 %copy-start.7 = (f32[8,512]{1,0:T(8,128)S(1)}, f32[8,512]{1,0:T(8,128)}, u32[]{:S(2)}) copy-start(f32[8,512]{1,0:T(8,128)} %bitcast_maximum_fusion.1) | copy-start | bytes 49156
  135.2 8.4 %copy-start.6 = (bf16[512,128]{1,0:T(8,128)(2,1)S(1)}, bf16[512,128]{1,0:T(8,128)(2,1)}, u32[]{:S(2)}) copy-start(bf16[512,128]{1,0:T(8,128)(2,1)} %param.13) | copy-start | bytes 393220
  138.3 5.3 copy-start.8
  138.3 5.3 copy-start.4
  143.6 5.7 %copy-start.1 = (bf16[1024,2048]{1,0:T(8,128)(2,1)S(1)}, bf16[1024,2048]{1,0:T(8,128)(2,1)}, u32[]{:S(2)}) copy-start(bf16[1024,2048]{1,0:T(8,128)(2,1)} %param.15) | copy-start | bytes 12582916
  149.3 4.4 copy-start.11
  153.7 3.2 copy-start.14
  153.7 3.3 copy-start.13
  153.7 50.1 %copy-start.9 = (f32[2048]{0:T(1024)S(1)}, f32[2048]{0:T(1024)}, u32[]{:S(2)}) copy-start(f32[2048]{0:T(1024)} %param.17) | copy-start | bytes 24580
  154.5 0.8 copy-start.2
  203.1 0.8 copy-start.3
  391.1 6.9 %copy-start.12 = (f32[128,8]{0,1:T(8,128)S(1)}, f32[128,8]{0,1:T(8,128)}, u32[]{:S(2)}) copy-start(f32[128,8]{0,1:T(8,128)} %param.21) | copy-start | bytes 12292
  391.1 108.4 %all-to-all-start.2 = ((bf16[128,16,2048]{2,1,0:T(8,128)(2,1)}), bf16[128,16,2048]{2,1,0:T(8,128)(2,1)}, u32[]{:S(2)}, u32[]{:S(2)}) async-start(bf16[128,16,2048]{2,1,0:T(8,128)(2,1)} %copy.52), calls=%async_computation.3 | async-start | bytes 16777216 | tf_op jit(solution)/shard_map/all_to_all | solution.py:120
Sparse Core Ops, SparseCore 0:
  153.9 47.5 reduce-scatter.1
